TPU v7x, 512 devices: a whole 4x8x8 slice. The times are simulated.
512 devices in a mesh: lon: 32 (over z_lo, y), lat: 16 (over z_hi, x, core).
Axes of the slice: x: 4, y: 8, z: 8 (z_hi: 2, z_lo: 4; z = z_hi * 4 + z_lo), core: 2. Of those that a mesh axis runs over, the one named last changes fastest.
Arguments:
- wind_u: float32 [720, 1440, 16], P('lat', 'lon'), may hold values from -6 to 6
- wind_v: float32 [720, 1440, 16], P('lat', 'lon'), may hold values from -6 to 6
- vorticity: float32 [720, 1440, 16], P('lat', 'lon'), may hold values from -6 to 6
- sample_level: int32 [16], replicated, may hold values from 0 to 1, as said below
- slot_wavenumber: int32 [736], P('lon'), may hold values from -1 to 719, as said below
- legendre_p: bfloat16 [720, 529920], P('lat', 'lon'), may hold values from -5 to 5
- legendre_h: bfloat16 [720, 529920], P('lat', 'lon'), may hold values from -5 to 5
Outputs:
- spectra: float32 [2, 529920], P(None, ('lon', 'lat'))
Inputs may be any that keep to these rules, and one draw needn't show every extreme that they name: `sample_level`: each level is named by exactly 8 samples. `slot_wavenumber`: each wavenumber from 0 to 719 stands in exactly one slot; the remaining slots hold -1.
All inputs are finite; a program needn't handle non-finite values.
Results may differ from a plain program's by a relative error of at most 0.0014.
Values sent between devices are 32-bit elements; how exact they have to be, the bound alone decides.
A program may use at most 128 MiB of HBM per device.

v0:
```python
import math

import jax
import jax.numpy as jnp
from jax import lax
from jax.sharding import PartitionSpec as P

NLON = 1440
NLAT = 720
MAXM = 720
LEV = 2
DAYS = 8
S = 16


def remove_means(field, onehot):
    means = jnp.einsum("jis,sl->jil", field, onehot, precision=lax.Precision.HIGHEST) / DAYS
    return field - jnp.einsum("jil,sl->jis", means, onehot, precision=lax.Precision.HIGHEST)


def fourier_table(waves, count):
    longitude = jnp.arange(count, dtype=jnp.int32)
    present = waves >= 0
    clipped = jnp.maximum(waves, 0)
    residue = longitude[:, None] * clipped[None, :] % NLON
    angle = residue.astype(jnp.float32) * (2.0 * math.pi / NLON)
    weight = present.astype(jnp.float32)[None, :] / NLON
    return jnp.stack([jnp.cos(angle) * weight, jnp.sin(angle) * weight], axis=2)


def body(wind_u, wind_v, vorticity, sample_level, slot_wavenumber, legendre_p, legendre_h):
    band_rows = wind_u.shape[0]
    lat_count = lax.axis_size("lat")
    onehot = (sample_level[:, None] == jnp.arange(LEV, dtype=jnp.int32)[None, :]).astype(
        jnp.float32
    )
    eddy_u = remove_means(wind_u, onehot)
    eddy_v = remove_means(wind_v, onehot)
    eddy_z = remove_means(vorticity, onehot)
    row_index = lax.axis_index("lat") * band_rows + jnp.arange(band_rows, dtype=jnp.int32)
    latitude = (row_index.astype(jnp.float32) + 0.5) * (math.pi / NLAT) - 0.5 * math.pi
    cosine = jnp.cos(latitude)[:, None, None]
    fluxes = jnp.concatenate([eddy_u * eddy_z * cosine, eddy_v * eddy_z * cosine], axis=2)
    owned_count = slot_wavenumber.shape[0]
    piece = lax.all_gather(fluxes, "lon", axis=1, tiled=True)
    table = fourier_table(slot_wavenumber, piece.shape[1])
    coeffs = jnp.einsum("jic,iqt->jqtc", piece, table, precision=lax.Precision.HIGHEST)
    present = slot_wavenumber >= 0
    clipped = jnp.maximum(slot_wavenumber, 0)
    scale = (clipped.astype(jnp.float32) / MAXM)[None, :, None]
    cos_u = coeffs[:, :, 0, :S]
    sin_u = coeffs[:, :, 1, :S]
    cos_v = coeffs[:, :, 0, S:]
    sin_v = coeffs[:, :, 1, S:]
    right_p = jnp.concatenate([scale * sin_u, scale * cos_u], axis=2).astype(jnp.bfloat16)
    right_h = jnp.concatenate([-cos_v, sin_v], axis=2).astype(jnp.bfloat16)
    table_p = legendre_p.reshape(band_rows, owned_count, MAXM)
    table_h = legendre_h.reshape(band_rows, owned_count, MAXM)
    partial_sum = jnp.einsum("jqn,jqc->qnc", table_p, right_p, preferred_element_type=jnp.float32)
    partial_sum = partial_sum + jnp.einsum(
        "jqn,jqc->qnc", table_h, right_h, preferred_element_type=jnp.float32
    )
    degree = jnp.arange(MAXM, dtype=jnp.int32)
    keep = ((degree[None, :] >= clipped[:, None]) & present[:, None]).astype(jnp.float32)
    flat_terms = (partial_sum * keep[:, :, None]).reshape(owned_count * MAXM, 2 * S)
    share = flat_terms.shape[0] // lat_count
    summed = lax.psum(flat_terms, "lat")
    mine = lax.dynamic_slice_in_dim(summed, lax.axis_index("lat") * share, share, 0)
    power = mine[:, :S] ** 2 + mine[:, S:] ** 2
    spectra = jnp.dot(power, onehot, precision=lax.Precision.HIGHEST) / DAYS
    return spectra.T


def solution(mesh):
    placed = (
        P("lat", "lon", None),
        P("lat", "lon", None),
        P("lat", "lon", None),
        P(),
        P("lon"),
        P("lat", "lon"),
        P("lat", "lon"),
    )
    return jax.shard_map(
        body, mesh=mesh, in_specs=placed, out_specs=P(None, ("lon", "lat")), check_vma=False
    )
```

profile of v0, /device:TPU:1, one launch (start us, length us, event | category | flops | bytes accessed | tf_op | source)
XLA Modules:
  0.0 525.2 jit_solution(9790209907816465756)
XLA Ops:
  6.5 0.0 copy-start.2
  6.5 0.0 copy-start
  6.5 0.0 copy-start.1
  6.5 0.0 all-gather.2.cloned.1.call-start
  6.6 1.3 fusion.16
  7.9 1.4 convolution_subtract_fusion.1
  9.3 1.2 fusion.15
  10.5 1.2 fusion.17
  11.8 0.0 copy-done
  11.8 1.1 fusion.13
  12.9 0.0 copy-done.2
  12.9 0.0 copy-done.1
  12.9 0.4 fusion.14
  13.3 0.1 pad_maximum_fusion
  13.4 1.7 copy.19
  15.1 0.0 all-gather.2.cloned.1.call-update
  15.1 0.2 all-reduce.2.cloned.1.call-start
  15.3 4.0 reshape.180
  19.3 0.0 copy-start.3
  19.3 4.0 reshape.179
  23.4 0.0 copy-done.3
  23.4 0.1 fusion.37
  23.5 1.4 cosine_multiply_fusion
  24.9 262.6 %all-gather.2.cloned.1.call-done = f32[45,1440,32]{0,2,1:T(8,128)} async-done(((f32[45,45,32]{0,2,1:T(8,128)}), f32[45,1440,32]{0,2,1:T(8,128)}) %all-gather.2.cloned.1.call-update) | async-done | bytes 8294416 | tf_op jit(solution)/shard_map/all_gather | solution.py:45
  287.4 17.4 %copy.20 = f32[45,1440,32]{1,0,2:T(8,128)} copy(f32[45,1440,32]{0,2,1:T(8,128)} %all-gather.2.cloned.1.call-done) | data formatting | bytes 16588800 | tf_op jit(solution)/shard_map/all_gather | solution.py:45
  304.8 18.9 %fusion.8 = f32[45,23,2,32]{0,1,3,2:T(8,128)S(1)} fusion(f32[45,1440,32]{1,0,2:T(8,128)} %copy.20, f32[1440,23,1]{0,1,2:T(8,128)} %get-tuple-element.8, f32[1440,23,1]{0,1,2:T(8,128)S(1)} %get-tuple-element.7), kind=kOutput, calls=%fused_computation.8 | convolution fusion | flops 1144693504 | bytes 8824320 | tf_op jit(solution)/shard_map/jic,iqt->jqtc/dot_general | solution.py:47
  323.7 0.1 fusion.24
  323.9 0.5 fusion.2
  324.4 0.6 multiply_bitcast_fusion
  325.0 1.3 copy.25
  326.3 2.0 reshape.181
  328.3 0.0 all-reduce.2.cloned.1.call-update
  328.4 188.2 %all-reduce.2.cloned.1.call-done = f32[16560,32]{0,1:T(8,128)} async-done(((f32[16560,32]{0,1:T(8,128)}), f32[16560,32]{0,1:T(8,128)}) %all-reduce.2.cloned.1.call-update) | async-done | bytes 2119696 | tf_op jit(solution)/shard_map/psum | solution.py:67
  516.6 1.8 convolution_multiply_fusion
  (8 shorter events, 0.2 us)
Async XLA Ops:
  6.5 6.3 %copy-start.2 = (s32[16]{0:T(128)S(1)}, s32[16]{0:T(128)}, u32[]{:S(2)}) copy-start(s32[16]{0:T(128)} %param.10) | copy-start | bytes 196
  6.5 5.3 %copy-start = (f32[45,45,16]{1,2,0:T(8,128)S(1)}, f32[45,45,16]{1,2,0:T(8,128)}, u32[]{:S(2)}) copy-start(f32[45,45,16]{1,2,0:T(8,128)} %param.8) | copy-start | bytes 388804
  6.5 6.3 %copy-start.1 = (f32[45,45,16]{1,2,0:T(8,128)S(1)}, f32[45,45,16]{1,2,0:T(8,128)}, u32[]{:S(2)}) copy-start(f32[45,45,16]{1,2,0:T(8,128)} %param.7) | copy-start | bytes 388804
  6.5 280.9 %all-gather.2.cloned.1.call-start = ((), (), s32[]{:S(2)}) async-start(), calls=%async_computation | async-start | bytes 24330240 | tf_op jit(solution)/shard_map/all_gather | solution.py:45
  15.1 501.5 %all-reduce.2.cloned.1.call-start = ((), (), s32[]{:S(2)}) async-start(), calls=%async_computation.1 | async-start | bytes 4259840 | tf_op jit(solution)/shard_map/psum | solution.py:67
  19.3 4.0 copy-start.3
Sparse Core Ops, SparseCore 0:
  15.2 272.1 all-gather.1
  328.5 188.0 all-reduce.1
where the time goes:
time: 526 us; the launch traced here: 525 us
  waiting for transfers between devices  451 us (86%)
  local copies, waits for them, and re-layouts  30.4 us (6%)
  matrix products  28.3 us (5%)
  between operations  13.6 us (3%)
    all_gather x1, waiting for transfers between devices, body(): piece = lax.all_gather(fluxes, 'lon', axis=1, tiled=True)  263 us
    psum x1, waiting for transfers between devices, body(): summed = lax.psum(flat_terms, 'lat')  188 us
    dot_general x1, matrix products, body(): jnp.einsum('jic,iqt->jqtc', piece, table, precision=lax.Precision.HIGHEST)  18.9 us
    all_gather x1, local copies, waits for them, and re-layouts, body(): piece = lax.all_gather(fluxes, 'lon', axis=1, tiled=True)  17.4 us
  transfers between devices with their start and end apart: 2, of which 2 were waited for; matrix products, arithmetic and copies ran while one was open for 2% of the time, Pallas kernels for 0%

commit v1 on v0

v1 whole, which is shorter than its diff:
```python
import math

import jax
import jax.numpy as jnp
from jax import lax
from jax.experimental import pallas as pl
from jax.experimental.pallas import tpu as pltpu
from jax.sharding import PartitionSpec as P

NLON = 1440
NLAT = 720
MAXM = 720
LEV = 2
DAYS = 8
S = 16

LON = 32
LAT = 16
BAND = NLAT // LAT
LOCAL = NLON // LON
OWN = 23
ROWS = 24
COLS = OWN * MAXM
SHARE = COLS // LAT
WIDE = 1152
STEP = 11

F32 = jnp.float32
BF16 = jnp.bfloat16
MESH = pl.DeviceIdType.MESH


def iota(shape, dim):
    return lax.broadcasted_iota(jnp.int32, shape, dim)


def roll64(value):
    return pltpu.roll(value, 64, 1)


def sincos(turns):
    quarter = jnp.floor(turns * (1.0 / 360.0) + 0.5)
    phi = (turns - 360.0 * quarter) * (2.0 * math.pi / NLON)
    sq = phi * phi
    s = phi * (1.0 + sq * (-1.0 / 6 + sq * (1.0 / 120 + sq * (-1.0 / 5040 + sq * (1.0 / 362880)))))
    c = 1.0 + sq * (-0.5 + sq * (1.0 / 24 + sq * (-1.0 / 720 + sq * (1.0 / 40320 - sq * (1.0 / 3628800)))))
    quad = quarter.astype(jnp.int32) & 3
    odd = (quad & 1) == 1
    cos = jnp.where(odd, s, c)
    sin = jnp.where(odd, c, s)
    cos = jnp.where((quad == 1) | (quad == 2), -cos, cos)
    sin = jnp.where(quad >= 2, -sin, sin)
    return cos, sin


def kernel(
    u_ref, v_ref, z_ref, level_ref, wave_ref, p_hbm, h_hbm, out_ref,
    p_ref, h_ref, flux, send1, recv1, wsend, wrecv,
    cos_hi, cos_lo, sin_hi, sin_lo, xs, send2, recv2, left_p, left_h,
    total, toward, held, got_core, got_a, got_b, plus, minus, final, got_z,
    load_sem, wsend_sem, wrecv_sem, send1_sem, recv1_sem, send2_sem, recv2_sem,
    core_send, core_recv, x_send, x_recv, z_send, z_recv,
):
    me = lax.axis_index("lon")
    lat = lax.axis_index("lat")
    core = lax.rem(lat, 2)
    x = lax.rem(lat // 2, 4)
    half = lat // 8

    def lat_at(h, xx, cc):
        return (h * 4 + xx) * 2 + cc

    partner = lat_at(half, x, 1 - core)
    up = lat_at(half, lax.rem(x + 1, 4), core)
    down = lat_at(half, lax.rem(x + 3, 4), core)
    across = lat_at(1 - half, x, core)

    def other(k):
        return lax.rem(me + STEP * k, LON)

    load_p = pltpu.make_async_copy(p_hbm, p_ref, load_sem.at[0])
    load_h = pltpu.make_async_copy(h_hbm, h_ref, load_sem.at[1])
    load_p.start()
    load_h.start()
    barrier = pltpu.get_barrier_semaphore()

    def greet(k, carry):
        pl.semaphore_signal(barrier, inc=1, device_id=(other(k), lat), device_id_type=MESH)
        return carry

    lax.fori_loop(1, LON, greet, 0)
    for there in (partner, up, down, across):
        pl.semaphore_signal(barrier, inc=1, device_id=(me, there), device_id_type=MESH)

    rows16 = iota((S, 128), 0)
    upper = jnp.zeros((S, 128), F32)
    for s in range(S):
        upper = jnp.where(rows16 == s, level_ref[s].astype(F32), upper)
    lower = 1.0 - upper
    upper45 = upper[None, :, :LOCAL]
    lower45 = lower[None, :, :LOCAL]
    flux[pl.ds(BAND * 32, 96), :] = jnp.zeros((96, 128), F32)
    STRIP = 9

    def eddies(strip, carry):
        at = strip * STRIP

        def eddy(ref):
            field = ref[pl.ds(at, STRIP)]
            one = jnp.sum(field * upper45, axis=1, keepdims=True)
            zero = jnp.sum(field * lower45, axis=1, keepdims=True)
            return field - (one * upper45 + zero * lower45) * (1.0 / DAYS)

        row = lat * BAND + at + iota((STRIP, 1, LOCAL), 0)
        theta = (row.astype(F32) + 0.5) * (math.pi / NLAT) - 0.5 * math.pi
        ez = eddy(z_ref) * jnp.cos(theta)
        fu = eddy(u_ref) * ez
        fv = eddy(v_ref) * ez
        for j in range(STRIP):
            base = pl.multiple_of((at + j) * 32, 32)
            flux[pl.ds(base, S), 0:LOCAL] = fu[j]
            flux[pl.ds(base + S, S), 0:LOCAL] = fv[j]
        return carry

    lax.fori_loop(0, BAND // STRIP, eddies, 0)

    lane1 = iota((1, 128), 1)
    waves = jnp.full((1, 128), -1.0, F32)
    for q in range(OWN):
        waves = jnp.where(lane1 == q, wave_ref[q].astype(F32), waves)
    wsend[...] = waves
    wrecv[me] = waves

    pl.semaphore_wait(barrier, LON - 1 + 4)

    def wave_copy(k, there):
        return pltpu.make_async_remote_copy(
            src_ref=wsend, dst_ref=wrecv.at[me],
            send_sem=wsend_sem.at[k], recv_sem=wrecv_sem.at[me],
            device_id=(there, lat), device_id_type=MESH,
        )

    def wave_start(k, carry):
        wave_copy(k, other(k)).start()
        return carry

    lax.fori_loop(1, LON, wave_start, 0)

    lane24 = iota((ROWS, 128), 1)
    low24 = lane24 < 64

    def message(c):
        first = flux[pl.ds(c, ROWS, stride=32), :]
        second = flux[pl.ds(c + ROWS * 32, ROWS, stride=32), :]
        packed = jnp.where(low24, first, roll64(second))
        return jnp.where((lane24 & 63) < LOCAL, packed, 0.0)

    def block(c):
        return pl.ds(pl.multiple_of(c * ROWS, 8), ROWS)

    def copy1(k, there):
        return pltpu.make_async_remote_copy(
            src_ref=send1.at[block(k)], dst_ref=recv1.at[block(me)],
            send_sem=send1_sem.at[k], recv_sem=recv1_sem.at[me],
            device_id=(there, lat), device_id_type=MESH,
        )

    def start1(k, carry):
        c = other(k)
        send1[block(k), :] = message(c)
        copy1(k, c).start()
        return carry

    lax.fori_loop(1, LON, start1, 0)
    recv1[block(me), :] = message(me)

    def wave_wait(k, carry):
        s = other(k)
        pltpu.make_async_remote_copy(
            src_ref=wsend, dst_ref=wrecv.at[s],
            send_sem=wsend_sem.at[k], recv_sem=wrecv_sem.at[s],
            device_id=(s, lat), device_id_type=MESH,
        ).wait()
        return carry

    lax.fori_loop(1, LON, wave_wait, 0)

    on_diagonal = iota((ROWS, 128), 0) == lane24

    def wave_column(s):
        row = jnp.broadcast_to(wrecv[s], (ROWS, 128))
        return jnp.sum(jnp.where(on_diagonal, row, 0.0), axis=1, keepdims=True)

    def split(value):
        high = value.astype(BF16)
        return high, (value - high.astype(F32)).astype(BF16)

    lane48 = iota((2 * ROWS, 128), 1)
    lon48 = ((lane48 & 63) + jnp.where(lane48 < 64, 0, LOCAL)).astype(F32)

    def tables(pair, carry):
        wave = jnp.concatenate([wave_column(2 * pair), wave_column(2 * pair + 1)], axis=0)
        wave = jnp.maximum(wave, 0.0)
        c, s = sincos(wave * lon48)
        rc, rs = sincos(jnp.broadcast_to(wave * (2.0 * LOCAL), (2 * ROWS, 128)))
        at = pl.ds(pl.multiple_of(pair * 2 * ROWS, 16), 2 * ROWS)
        for j in range(8):
            lanes = slice(128 * j, 128 * (j + 1))
            ch, cl = split(c)
            sh, sl = split(s)
            cos_hi[at, lanes] = ch
            cos_lo[at, lanes] = cl
            sin_hi[at, lanes] = sh
            sin_lo[at, lanes] = sl
            c, s = c * rc - s * rs, s * rc + c * rs
        return carry

    lax.fori_loop(0, LON // 2, tables, 0)

    def wait1(k, carry):
        s = other(k)
        pltpu.make_async_remote_copy(
            src_ref=send1.at[block(k)], dst_ref=recv1.at[block(s)],
            send_sem=send1_sem.at[k], recv_sem=recv1_sem.at[s],
            device_id=(s, lat), device_id_type=MESH,
        ).wait()
        return carry

    lax.fori_loop(1, LON, wait1, 0)

    pad = jnp.zeros((16, 128), F32)
    for h in range(2):
        for j in range(8):
            a = recv1[ROWS * (16 * h + 2 * j):ROWS * (16 * h + 2 * j + 1), :]
            b = recv1[ROWS * (16 * h + 2 * j + 1):ROWS * (16 * h + 2 * j + 2), :]
            piece = jnp.concatenate(
                [jnp.where(low24, a, roll64(b)), jnp.where(low24, roll64(a), b), pad], axis=0
            )
            high, low = split(piece)
            xs[64 * h:64 * h + 64, 128 * j:128 * (j + 1)] = high
            xs[128 + 64 * h:192 + 64 * h, 128 * j:128 * (j + 1)] = low

    is_v = me >= S
    nt = (((1,), (1,)), ((), ()))
    PART = 384
    lane_part = iota((PART, 128), 1)
    low_part = lane_part < 64

    def copy2(k, there):
        return pltpu.make_async_remote_copy(
            src_ref=send2.at[block(there)], dst_ref=recv2.at[block(me)],
            send_sem=send2_sem.at[k], recv_sem=recv2_sem.at[me],
            device_id=(there, lat), device_id_type=MESH,
        )

    for part in range(LON * ROWS // PART):
        at = slice(part * PART, (part + 1) * PART)

        def transform(high_ref, low_ref):
            wide = lax.dot_general(high_ref[at, :], xs[...], nt, preferred_element_type=F32)
            thin = lax.dot_general(low_ref[at, :], xs[0:128, :], nt, preferred_element_type=F32)
            return wide[:, :128] + wide[:, 128:] + thin

        c = transform(cos_hi, cos_lo)
        s = transform(sin_hi, sin_lo)
        wave = jnp.concatenate(
            [wave_column(i) for i in range(part * PART // ROWS, (part + 1) * PART // ROWS)], axis=0
        )
        clipped = jnp.maximum(wave, 0.0)
        present = jnp.where(wave >= 0.0, 1.0 / NLON, 0.0)
        sign = 1.0 - 2.0 * (clipped - 2.0 * jnp.floor(clipped * 0.5))
        scale = clipped * (1.0 / MAXM) * present
        sin_scale = jnp.where(is_v, present, scale)
        cos_scale = jnp.where(is_v, -present, scale)
        near = jnp.where(low_part, s, roll64(c))
        far = jnp.where(low_part, roll64(s), c)
        near = jnp.where(low_part, s, roll64(c))
        send2[at, :] = (near + sign * far) * jnp.where(low_part, sin_scale, cos_scale)

    def start2(k, carry):
        copy2(k, other(k)).start()
        return carry

    lax.fori_loop(1, LON, start2, 0)
    recv2[block(me), :] = send2[block(me), :]

    def wait2(k, carry):
        s = other(k)
        pltpu.make_async_remote_copy(
            src_ref=send2.at[block(s)], dst_ref=recv2.at[block(s)],
            send_sem=send2_sem.at[k], recv_sem=recv2_sem.at[s],
            device_id=(s, lat), device_id_type=MESH,
        ).wait()
        return carry

    lax.fori_loop(1, LON, wait2, 0)

    def sides(q, carry):
        wu = recv2[pl.ds(q, S, stride=ROWS), :]
        wv = recv2[pl.ds(q + S * ROWS, S, stride=ROWS), :]
        at = pl.ds(pl.multiple_of(q * 32, 32), 32)
        left_p[at, :] = jnp.concatenate([wu, roll64(wu)], axis=0).astype(BF16)
        left_h[at, :] = jnp.concatenate([roll64(wv), wv], axis=0).astype(BF16)
        return carry

    lax.fori_loop(0, ROWS, sides, 0)
    load_p.wait()
    load_h.wait()

    def legendre(base, q, cols):
        rows = pl.ds(pl.multiple_of(q * 32, 32), 64)
        r = jnp.dot(left_p[rows, 0:BAND], p_ref[:, cols], preferred_element_type=F32)
        r = r + jnp.dot(left_h[rows, 0:BAND], h_ref[:, cols], preferred_element_type=F32)
        inside = iota((32, r.shape[1]), 1) < MAXM * (q + 1) - base
        return jnp.where(inside, r[:32], r[32:])

    TILE = 256

    def sums(t, carry):
        base = t * TILE
        cols = pl.ds(pl.multiple_of(base, TILE), TILE)
        total[:, cols] = legendre(base, base // MAXM, cols)
        return carry

    whole = COLS // TILE
    lax.fori_loop(0, whole, sums, 0, unroll=4)
    last = slice(whole * TILE, COLS)
    total[:, last] = legendre(whole * TILE, OWN - 1, last)

    lane32 = iota((32, 128), 1)

    def chunk(b):
        first = SHARE * b
        tile = first // 128
        shift = first - tile * 128
        back = lax.rem(128 - shift, 128)
        inside = lane32 < 128 - shift
        turned = [
            pltpu.roll(total[:, pl.ds(pl.multiple_of((tile + i) * 128, 128), 128)], back, 1)
            for i in range(10)
        ]
        return [jnp.where(inside, turned[i], turned[i + 1]) for i in range(9)]

    order = [(1, 2), (1, 1), (1, 3), (1, 0), (0, 2), (0, 1), (0, 3), (0, 0)]
    place = {pair: i for i, pair in enumerate(order)}

    def target(pair, cc):
        dz, dx = pair
        return lat_at(half if dz == 0 else 1 - half, lax.rem(x + dx, 4), cc)

    def send(src, dst, sends, recvs, i, there):
        return pltpu.make_async_remote_copy(
            src_ref=src, dst_ref=dst, send_sem=sends.at[i], recv_sem=recvs.at[i],
            device_id=(me, there), device_id_type=MESH,
        )

    core_copies = []
    for i, pair in enumerate(order):
        pieces = chunk(target(pair, 1 - core))
        for n in range(9):
            toward[i, :, 128 * n:128 * (n + 1)] = pieces[n]
        copy = send(toward.at[i], got_core.at[i], core_send, core_recv, i, partner)
        copy.start()
        core_copies.append(copy)

    A, B = slice(0, 16), slice(16, 32)
    x_copies = {}

    def x_start(i, src, dst, there):
        copy = send(src, dst, x_send, x_recv, i, there)
        copy.start()
        x_copies[i] = copy

    def merge(pair):
        i = place[pair]
        pieces = chunk(target(pair, core))
        core_copies[i].wait()
        for n in range(9):
            lanes = slice(128 * n, 128 * (n + 1))
            held[i, :, lanes] = pieces[n] + got_core[i, :, lanes]

    for dz in (1, 0):
        k = 6 * dz
        merge((dz, 2))
        i = place[(dz, 2)]
        x_start(k, held.at[i, A], got_a.at[dz], up)
        x_start(k + 1, held.at[i, B], got_b.at[dz], down)
        merge((dz, 1))
        x_start(k + 2, held.at[place[(dz, 1)], B], plus.at[dz, B], up)
        merge((dz, 3))
        x_start(k + 3, held.at[place[(dz, 3)], A], minus.at[dz, A], down)
        merge((dz, 0))
    z_copies = []
    for dz in (1, 0):
        k = 6 * dz
        i, j, own = place[(dz, 1)], place[(dz, 3)], place[(dz, 0)]
        x_copies[k].wait()
        held[i, A] = held[i, A] + got_a[dz]
        x_start(k + 4, held.at[i, A], plus.at[dz, A], up)
        x_copies[k + 1].wait()
        held[j, B] = held[j, B] + got_b[dz]
        x_start(k + 5, held.at[j, B], minus.at[dz, B], down)
    for dz in (1, 0):
        k = 6 * dz
        own = place[(dz, 0)]
        x_copies[k + 4].wait()
        x_copies[k + 3].wait()
        final[dz, A] = held[own, A] + plus[dz, A] + minus[dz, A]
        if dz == 1:
            copy = send(final.at[1, A], got_z.at[A], z_send, z_recv, 0, across)
            copy.start()
            z_copies.append(copy)
        x_copies[k + 5].wait()
        x_copies[k + 2].wait()
        final[dz, B] = held[own, B] + plus[dz, B] + minus[dz, B]
        if dz == 1:
            copy = send(final.at[1, B], got_z.at[B], z_send, z_recv, 1, across)
            copy.start()
            z_copies.append(copy)
    for copy in z_copies:
        copy.wait()

    first = lat * SHARE
    slot = first // MAXM
    lane = first + iota((1, WIDE), 1)
    keep = jnp.zeros((1, WIDE), F32)
    for d in range(3):
        q = jnp.minimum(slot + d, OWN - 1)
        wave = wave_ref[q]
        n = lane - (slot + d) * MAXM
        good = (n >= 0) & (n < MAXM) & (n >= wave) & (wave >= 0)
        keep = jnp.where(good, 1.0, keep)
    re = final[0, A] + got_z[A]
    im = final[0, B] + got_z[B]
    power = re * re + im * im
    one = jnp.sum(power * upper[:, :1], axis=0, keepdims=True)
    zero = jnp.sum(power * lower[:, :1], axis=0, keepdims=True)
    keep = keep * (1.0 / DAYS)
    out_ref[0:1, :] = (zero * keep)[:, :SHARE]
    out_ref[1:2, :] = (one * keep)[:, :SHARE]


def body(wind_u, wind_v, vorticity, sample_level, slot_wavenumber, legendre_p, legendre_h):
    def turned(field):
        return jnp.transpose(field, (0, 2, 1))

    vmem = pl.BlockSpec(memory_space=pltpu.VMEM)
    smem = pl.BlockSpec(memory_space=pltpu.SMEM)
    hbm = pl.BlockSpec(memory_space=pl.ANY)
    dma = pltpu.SemaphoreType.DMA
    scratch = [
        pltpu.VMEM((BAND, COLS), BF16),
        pltpu.VMEM((BAND, COLS), BF16),
        pltpu.VMEM((48 * 32, 128), F32),
        pltpu.VMEM((LON * ROWS, 128), F32),
        pltpu.VMEM((LON * ROWS, 128), F32),
        pltpu.VMEM((1, 128), F32),
        pltpu.VMEM((LON, 1, 128), F32),
        pltpu.VMEM((LON * ROWS, 1024), BF16),
        pltpu.VMEM((LON * ROWS, 1024), BF16),
        pltpu.VMEM((LON * ROWS, 1024), BF16),
        pltpu.VMEM((LON * ROWS, 1024), BF16),
        pltpu.VMEM((256, 1024), BF16),
        pltpu.VMEM((LON * ROWS, 128), F32),
        pltpu.VMEM((LON * ROWS, 128), F32),
        pltpu.VMEM((ROWS * 32, 128), BF16),
        pltpu.VMEM((ROWS * 32, 128), BF16),
        pltpu.VMEM((32, 131 * 128), F32),
        pltpu.VMEM((8, 32, WIDE), F32),
        pltpu.VMEM((8, 32, WIDE), F32),
        pltpu.VMEM((8, 32, WIDE), F32),
        pltpu.VMEM((2, 16, WIDE), F32),
        pltpu.VMEM((2, 16, WIDE), F32),
        pltpu.VMEM((2, 32, WIDE), F32),
        pltpu.VMEM((2, 32, WIDE), F32),
        pltpu.VMEM((2, 32, WIDE), F32),
        pltpu.VMEM((32, WIDE), F32),
        dma((2,)),
        dma((LON,)), dma((LON,)), dma((LON,)), dma((LON,)), dma((LON,)), dma((LON,)),
        dma((8,)), dma((8,)), dma((12,)), dma((12,)), dma((2,)), dma((2,)),
    ]
    return pl.pallas_call(
        kernel,
        out_shape=jax.ShapeDtypeStruct((LEV, SHARE), F32),
        in_specs=[vmem, vmem, vmem, smem, smem, hbm, hbm],
        out_specs=vmem,
        scratch_shapes=scratch,
        compiler_params=pltpu.CompilerParams(
            collective_id=0, has_side_effects=True, vmem_limit_bytes=60 * 1024 * 1024
        ),
    )(turned(wind_u), turned(wind_v), turned(vorticity), sample_level, slot_wavenumber,
      legendre_p, legendre_h)


def solution(mesh):
    placed = (
        P("lat", "lon", None),
        P("lat", "lon", None),
        P("lat", "lon", None),
        P(),
        P("lon"),
        P("lat", "lon"),
        P("lat", "lon"),
    )
    return jax.shard_map(
        body, mesh=mesh, in_specs=placed, out_specs=P(None, ("lon", "lat")), check_vma=False
    )
```

time: 526 us -> 73.7 us (0.14)
  the two profiles are of different devices: /device:TPU:1 before, /device:TPU:72 now
where the time goes in v1:
time: 73.7 us; the launch traced here: 73.5 us
  Pallas kernels  72.2 us (98%)
  local copies, waits for them, and re-layouts  1.3 us (2%)
    pallas_call x1, Pallas kernels, body(): pl.pallas_call(kernel, out_shape=jax.ShapeDtypeStruct((LEV, SHARE), F32),...  72.2 us

profile of v1, /device:TPU:72, one launch (start us, length us, event | category | flops | bytes accessed | tf_op | source)
XLA Modules:
  0.0 73.5 jit_solution(14287505829400211416)
XLA Ops:
  0.0 72.2 %shard_map.73 = f32[2,1035]{1,0:T(2,128)} custom-call(f32[45,16,45]{2,1,0:T(8,128)} %bitcast.3, f32[45,16,45]{2,1,0:T(8,128)} %bitcast.4, f32[45,16,45]{2,1,0:T(8,128)} %bitcast.5, s32[16]{0:T(128)} %level_ref.1, s32[23]{0:T(128)} %wave_ref.1, bf16[45,16560]{1,0:T(8,128)(2,1)} %p_hbm.1, bf16[45,16560]{1,0:T(8,128)(2,1)} %h_hbm.1), custom_call_target="tpu_custom_call" | custom-call | tf_op jit(solution)/shard_map/pallas_call | solution.py:482
  72.2 1.3 %copy.9 = f32[2,1035]{1,0:T(2,128)} copy(f32[2,1035]{1,0:T(2,128)} %shard_map.73) | data formatting | bytes 16560

commit v2 on v1

v2 whole, which is shorter than its diff:
```python
import math

import jax
import jax.numpy as jnp
from jax import lax
from jax.experimental import pallas as pl
from jax.experimental.pallas import tpu as pltpu
from jax.sharding import PartitionSpec as P

NLON = 1440
NLAT = 720
MAXM = 720
LEV = 2
DAYS = 8
S = 16

LON = 32
LAT = 16
BAND = NLAT // LAT
LOCAL = NLON // LON
OWN = 23
IN_ROWS = 16
OUT_ROWS = 17
SPACE = 24
COLS = OWN * MAXM
SHARE = COLS // LAT
WIDE = 1152
STEP = 11

F32 = jnp.float32
BF16 = jnp.bfloat16
MESH = pl.DeviceIdType.MESH


def iota(shape, dim):
    return lax.broadcasted_iota(jnp.int32, shape, dim)


def roll64(value):
    return pltpu.roll(value, 64, 1)


def sincos(turns):
    quarter = jnp.floor(turns * (1.0 / 360.0) + 0.5)
    phi = (turns - 360.0 * quarter) * (2.0 * math.pi / NLON)
    sq = phi * phi
    s = phi * (1.0 + sq * (-1.0 / 6 + sq * (1.0 / 120 + sq * (-1.0 / 5040 + sq * (1.0 / 362880)))))
    c = 1.0 + sq * (-0.5 + sq * (1.0 / 24 + sq * (-1.0 / 720 + sq * (1.0 / 40320 - sq * (1.0 / 3628800)))))
    quad = quarter.astype(jnp.int32) & 3
    odd = (quad & 1) == 1
    cos = jnp.where(odd, s, c)
    sin = jnp.where(odd, c, s)
    cos = jnp.where((quad == 1) | (quad == 2), -cos, cos)
    sin = jnp.where(quad >= 2, -sin, sin)
    return cos, sin


def packed(source, blocks, j):
    lane = iota((32, 128), 1)
    tile = jnp.zeros((32, 128), F32)
    for t in range(blocks):
        at = t * BAND - 128 * j
        if at >= 128 or at + BAND <= 0:
            continue
        value, start = source(t)
        shift = (at - start) % 128
        value = pltpu.roll(value, shift, 1) if shift else value
        tile = jnp.where((lane >= at) & (lane < at + BAND), value, tile)
    return tile


def unpacked(tile, t):
    lane = iota((32, 128), 1)
    j, at = divmod(t * BAND, 128)
    if at == 0:
        return tile(j)
    value = pltpu.roll(tile(j), 128 - at, 1)
    if at + BAND > 128:
        value = jnp.where(lane < 128 - at, value, pltpu.roll(tile(j + 1), 128 - at, 1))
    return value


def kernel(
    u_ref, v_ref, z_ref, level_ref, wave_ref, p_hbm, h_hbm, out_ref,
    p_ref, h_ref, wide_p, wide_h, flux, row1, send1, recv1, wsend, wrecv,
    cos_hi, cos_lo, sin_hi, sin_lo, field, xs, coeff, row2, send2, recv2, left_p, left_h,
    toward, held, got_core, got_a, got_b, plus, minus, final, got_z,
    load_sem, wsend_sem, wrecv_sem, send1_sem, recv1_sem, send2_sem, recv2_sem,
    core_send, core_recv, x_send, x_recv, z_send, z_recv,
):
    me = lax.axis_index("lon")
    lat = lax.axis_index("lat")
    core = lax.rem(lat, 2)
    x = lax.rem(lat // 2, 4)
    half = lat // 8

    def lat_at(h, xx, cc):
        return (h * 4 + xx) * 2 + cc

    partner = lat_at(half, x, 1 - core)
    up = lat_at(half, lax.rem(x + 1, 4), core)
    down = lat_at(half, lax.rem(x + 3, 4), core)
    across = lat_at(1 - half, x, core)

    def other(k):
        return lax.rem(me + STEP * k, LON)

    load_p = pltpu.make_async_copy(p_hbm, p_ref, load_sem.at[0])
    load_h = pltpu.make_async_copy(h_hbm, h_ref, load_sem.at[1])
    load_p.start()
    load_h.start()
    barrier = pltpu.get_barrier_semaphore()

    def greet(k, carry):
        pl.semaphore_signal(barrier, inc=1, device_id=(other(k), lat), device_id_type=MESH)
        return carry

    lax.fori_loop(1, LON, greet, 0)
    for there in (partner, up, down, across):
        pl.semaphore_signal(barrier, inc=1, device_id=(me, there), device_id_type=MESH)

    rows16 = iota((S, 128), 0)
    upper = jnp.zeros((S, 128), F32)
    for s in range(S):
        upper = jnp.where(rows16 == s, level_ref[s].astype(F32), upper)
    lower = 1.0 - upper
    upper45 = upper[None, :, :LOCAL]
    lower45 = lower[None, :, :LOCAL]
    STRIP = 9

    def eddies(strip, carry):
        at = strip * STRIP

        def eddy(ref):
            value = ref[pl.ds(at, STRIP)]
            one = jnp.sum(value * upper45, axis=1, keepdims=True)
            zero = jnp.sum(value * lower45, axis=1, keepdims=True)
            return value - (one * upper45 + zero * lower45) * (1.0 / DAYS)

        row = lat * BAND + at + iota((STRIP, 1, LOCAL), 0)
        theta = (row.astype(F32) + 0.5) * (math.pi / NLAT) - 0.5 * math.pi
        ez = eddy(z_ref) * jnp.cos(theta)
        fu = eddy(u_ref) * ez
        fv = eddy(v_ref) * ez
        for j in range(STRIP):
            base = pl.multiple_of((at + j) * 32, 32)
            flux[pl.ds(base, S), 0:LOCAL] = fu[j]
            flux[pl.ds(base + S, S), 0:LOCAL] = fv[j]
        return carry

    lax.fori_loop(0, BAND // STRIP, eddies, 0)

    for j in range(IN_ROWS):
        row1[32 * j:32 * j + 32, :] = packed(lambda t: (flux[32 * t:32 * t + 32, :], 0), BAND, j)

    lane1 = iota((1, 128), 1)
    waves = jnp.full((1, 128), -1.0, F32)
    for q in range(OWN):
        waves = jnp.where(lane1 == q, wave_ref[q].astype(F32), waves)
    wsend[...] = waves
    wrecv[pl.ds(me, 1), :] = waves

    pl.semaphore_wait(barrier, LON - 1 + 4)

    def wave_copy(k, there, source):
        return pltpu.make_async_remote_copy(
            src_ref=wsend, dst_ref=wrecv.at[pl.ds(source, 1)],
            send_sem=wsend_sem.at[k], recv_sem=wrecv_sem.at[source],
            device_id=(there, lat), device_id_type=MESH,
        )

    def wave_start(k, carry):
        wave_copy(k, other(k), me).start()
        return carry

    lax.fori_loop(1, LON, wave_start, 0)

    def in_block(c):
        return pl.ds(pl.multiple_of(c * IN_ROWS, 8), IN_ROWS)

    def copy1(k, there, source):
        return pltpu.make_async_remote_copy(
            src_ref=send1.at[in_block(k)], dst_ref=recv1.at[in_block(source)],
            send_sem=send1_sem.at[k], recv_sem=recv1_sem.at[source],
            device_id=(there, lat), device_id_type=MESH,
        )

    def start1(k, carry):
        c = other(k)
        send1[in_block(k), :] = row1[pl.ds(c, IN_ROWS, stride=32), :]
        copy1(k, c, me).start()
        return carry

    lax.fori_loop(1, LON, start1, 0)
    recv1[in_block(me), :] = row1[pl.ds(me, IN_ROWS, stride=32), :]

    load_p.wait()
    load_h.wait()
    PIECE = 2048

    def widen(i, carry):
        cols = pl.ds(pl.multiple_of(i * PIECE, PIECE), PIECE)
        wide_p[:, cols] = p_ref[:, cols]
        wide_h[:, cols] = h_ref[:, cols]
        return carry

    lax.fori_loop(0, COLS // PIECE, widen, 0)
    rest = slice(COLS // PIECE * PIECE, COLS)
    wide_p[:, rest] = p_ref[:, rest]
    wide_h[:, rest] = h_ref[:, rest]

    def wave_wait(k, carry):
        wave_copy(k, other(k), other(k)).wait()
        return carry

    lax.fori_loop(1, LON, wave_wait, 0)
    lane32 = iota((32, 128), 1)

    def wave_column(q):
        return jnp.sum(jnp.where(lane32 == q, wrecv[...], 0.0), axis=1, keepdims=True)

    def split(value):
        high = value.astype(BF16)
        return high, (value - high.astype(F32)).astype(BF16)

    lon32 = ((lane32 & 63) + jnp.where(lane32 < 64, 0, LOCAL)).astype(F32)

    def tables(q, carry):
        wave = jnp.maximum(wave_column(q), 0.0)
        c, s = sincos(wave * lon32)
        rc, rs = sincos(jnp.broadcast_to(wave * (2.0 * LOCAL), (32, 128)))
        at = pl.ds(pl.multiple_of(q * 32, 32), 32)
        for j in range(8):
            lanes = slice(128 * j, 128 * (j + 1))
            ch, cl = split(c)
            sh, sl = split(s)
            cos_hi[at, lanes] = ch
            cos_lo[at, lanes] = cl
            sin_hi[at, lanes] = sh
            sin_lo[at, lanes] = sl
            c, s = c * rc - s * rs, s * rc + c * rs
        return carry

    lax.fori_loop(0, OWN, tables, 0)

    def wait1(k, carry):
        copy1(k, other(k), other(k)).wait()
        return carry

    lax.fori_loop(1, LON, wait1, 0)

    row_tile = {}

    def in_tile(j):
        if j not in row_tile:
            row_tile[j] = recv1[pl.ds(j, LON, stride=IN_ROWS), :]
        return row_tile[j]

    for t in range(BAND):
        field[pl.ds(t, LON, stride=48), :] = unpacked(in_tile, t)

    lane48 = iota((48, 128), 1)
    west = lane48 < LOCAL
    east = (lane48 >= 64) & (lane48 < 64 + LOCAL)
    for h in range(2):
        for j in range(8):
            s = 16 * h + 2 * j
            a = field[48 * s:48 * s + 48, :]
            b = field[48 * s + 48:48 * s + 96, :]
            high, low = split(jnp.where(west, a, jnp.where(east, roll64(b), 0.0)))
            lanes = slice(128 * j, 128 * (j + 1))
            xs[64 * h:64 * h + 48, lanes] = high
            xs[128 + 64 * h:176 + 64 * h, lanes] = low

    is_v = me >= S
    nt = (((1,), (1,)), ((), ()))
    for first, count in ((0, 8), (8, 8), (16, 7)):
        size = count * 32
        at = slice(first * 32, first * 32 + size)
        low_part = iota((size, 128), 1) < 64

        def transform(high_ref, low_ref):
            wide = lax.dot_general(high_ref[at, :], xs[...], nt, preferred_element_type=F32)
            thin = lax.dot_general(low_ref[at, :], xs[0:128, :], nt, preferred_element_type=F32)
            return wide[:, :128] + wide[:, 128:] + thin

        c = transform(cos_hi, cos_lo)
        s = transform(sin_hi, sin_lo)
        wave = jnp.concatenate([wave_column(q) for q in range(first, first + count)], axis=0)
        clipped = jnp.maximum(wave, 0.0)
        present = jnp.where(wave >= 0.0, 1.0 / NLON, 0.0)
        sign = 1.0 - 2.0 * (clipped - 2.0 * jnp.floor(clipped * 0.5))
        scale = clipped * (1.0 / MAXM) * present
        sin_scale = jnp.where(is_v, present, scale)
        cos_scale = jnp.where(is_v, -present, scale)
        near = jnp.where(low_part, s, roll64(c))
        far = jnp.where(low_part, roll64(s), c)
        coeff[at, :] = (near + sign * far) * jnp.where(low_part, sin_scale, cos_scale)

    for j in range(OUT_ROWS):
        row2[32 * j:32 * j + 32, :] = packed(
            lambda t: (coeff[32 * (t // 2):32 * (t // 2) + 32, :], 64 * (t % 2)), 2 * OWN, j
        )

    def out_block(c):
        return pl.ds(pl.multiple_of(c * SPACE, 8), OUT_ROWS)

    def copy2(k, there, source):
        return pltpu.make_async_remote_copy(
            src_ref=send2.at[out_block(k)], dst_ref=recv2.at[out_block(source)],
            send_sem=send2_sem.at[k], recv_sem=recv2_sem.at[source],
            device_id=(there, lat), device_id_type=MESH,
        )

    def start2(k, carry):
        o = other(k)
        send2[out_block(k), :] = row2[pl.ds(o, OUT_ROWS, stride=32), :]
        copy2(k, o, me).start()
        return carry

    lax.fori_loop(1, LON, start2, 0)
    recv2[out_block(me), :] = row2[pl.ds(me, OUT_ROWS, stride=32), :]

    def wait2(k, carry):
        copy2(k, other(k), other(k)).wait()
        return carry

    lax.fori_loop(1, LON, wait2, 0)

    out_tiles = {}

    def out_tile(j):
        if j not in out_tiles:
            out_tiles[j] = recv2[pl.ds(j, LON, stride=SPACE), :]
        return out_tiles[j]

    for q in range(OWN):
        sin = unpacked(out_tile, 2 * q).astype(BF16)
        cos = unpacked(out_tile, 2 * q + 1).astype(BF16)
        at = slice(32 * q, 32 * q + 32)
        left_p[at, :] = jnp.concatenate([sin[:S], cos[:S]], axis=0)
        left_h[at, :] = jnp.concatenate([cos[S:], sin[S:]], axis=0)

    lane256 = iota((32, 256), 1)

    def chunk(b):
        first = SHARE * b
        tile = first // 128
        shift = first - tile * 128
        back = lax.rem(128 - shift, 128)
        inside = lane32 < 128 - shift
        turned = []
        for i in range(5):
            base = tile * 128 + 256 * i
            q = base // MAXM
            rows = pl.ds(pl.multiple_of(q * 32, 32), 64)
            cols = pl.ds(pl.multiple_of(base, 128), 256)
            r = jnp.dot(left_p[rows, 0:BAND], wide_p[:, cols], preferred_element_type=F32)
            r = r + jnp.dot(left_h[rows, 0:BAND], wide_h[:, cols], preferred_element_type=F32)
            r = jnp.where(lane256 < MAXM * (q + 1) - base, r[:32], r[32:])
            turned += [pltpu.roll(r[:, :128], back, 1), pltpu.roll(r[:, 128:], back, 1)]
        return [jnp.where(inside, turned[i], turned[i + 1]) for i in range(9)]

    order = [(1, 2), (1, 1), (1, 3), (0, 2), (1, 0), (0, 1), (0, 3), (0, 0)]
    place = {pair: i for i, pair in enumerate(order)}

    def target(pair, cc):
        dz, dx = pair
        return lat_at(half if dz == 0 else 1 - half, lax.rem(x + dx, 4), cc)

    def send(src, dst, sends, recvs, i, there):
        return pltpu.make_async_remote_copy(
            src_ref=src, dst_ref=dst, send_sem=sends.at[i], recv_sem=recvs.at[i],
            device_id=(me, there), device_id_type=MESH,
        )

    core_copies = {}

    def give(i):
        pieces = chunk(target(order[i], 1 - core))
        for n in range(9):
            toward[i, :, 128 * n:128 * (n + 1)] = pieces[n]
        core_copies[i] = send(toward.at[i], got_core.at[i], core_send, core_recv, i, partner)
        core_copies[i].start()

    def keep_own(i):
        pieces = chunk(target(order[i], core))
        for n in range(9):
            held[i, :, 128 * n:128 * (n + 1)] = pieces[n]

    def merge(i):
        core_copies[i].wait()
        held[i] = held[i] + got_core[i]

    A, B = slice(0, 16), slice(16, 32)
    x_copies = {}

    def x_start(i, src, dst, there):
        x_copies[i] = send(src, dst, x_send, x_recv, i, there)
        x_copies[i].start()

    def far_start(dz):
        i = place[(dz, 2)]
        x_start(6 * dz, held.at[i, A], got_a.at[dz], up)
        x_start(6 * dz + 1, held.at[i, B], got_b.at[dz], down)

    def near_start(dz):
        x_start(6 * dz + 2, held.at[place[(dz, 1)], B], plus.at[dz, B], up)
        x_start(6 * dz + 3, held.at[place[(dz, 3)], A], minus.at[dz, A], down)

    def relay(dz):
        i, j = place[(dz, 1)], place[(dz, 3)]
        x_copies[6 * dz].wait()
        held[i, A] = held[i, A] + got_a[dz]
        x_start(6 * dz + 4, held.at[i, A], plus.at[dz, A], up)
        x_copies[6 * dz + 1].wait()
        held[j, B] = held[j, B] + got_b[dz]
        x_start(6 * dz + 5, held.at[j, B], minus.at[dz, B], down)

    def finish(dz, part, one, two):
        own = place[(dz, 0)]
        x_copies[6 * dz + one].wait()
        x_copies[6 * dz + two].wait()
        final[dz, part] = held[own, part] + plus[dz, part] + minus[dz, part]

    for i in range(4):
        give(i)
    keep_own(0)
    merge(0)
    far_start(1)
    keep_own(1)
    merge(1)
    keep_own(2)
    merge(2)
    near_start(1)
    for i in range(4, 8):
        give(i)
    keep_own(3)
    keep_own(4)
    relay(1)
    merge(3)
    far_start(0)
    merge(4)
    keep_own(5)
    merge(5)
    keep_own(6)
    merge(6)
    near_start(0)
    keep_own(7)
    merge(7)
    finish(1, A, 3, 4)
    z_a = send(final.at[1, A], got_z.at[A], z_send, z_recv, 0, across)
    z_a.start()
    finish(1, B, 2, 5)
    z_b = send(final.at[1, B], got_z.at[B], z_send, z_recv, 1, across)
    z_b.start()
    relay(0)
    finish(0, A, 3, 4)
    finish(0, B, 2, 5)

    first = lat * SHARE
    slot = first // MAXM
    lane = first + iota((1, WIDE), 1)
    keep = jnp.zeros((1, WIDE), F32)
    for d in range(3):
        q = jnp.minimum(slot + d, OWN - 1)
        wave = wave_ref[q]
        n = lane - (slot + d) * MAXM
        good = (n >= 0) & (n < MAXM) & (n >= wave) & (wave >= 0)
        keep = jnp.where(good, 1.0 / DAYS, keep)
    z_a.wait()
    re = final[0, A] + got_z[A]
    z_b.wait()
    im = final[0, B] + got_z[B]
    power = re * re + im * im
    one = jnp.sum(power * upper[:, :1], axis=0, keepdims=True)
    zero = jnp.sum(power * lower[:, :1], axis=0, keepdims=True)
    out_ref[0:1, :] = (zero * keep)[:, :SHARE]
    out_ref[1:2, :] = (one * keep)[:, :SHARE]


def body(wind_u, wind_v, vorticity, sample_level, slot_wavenumber, legendre_p, legendre_h):
    def turned(field):
        return jnp.transpose(field, (0, 2, 1))

    vmem = pl.BlockSpec(memory_space=pltpu.VMEM)
    smem = pl.BlockSpec(memory_space=pltpu.SMEM)
    hbm = pl.BlockSpec(memory_space=pl.ANY)
    dma = pltpu.SemaphoreType.DMA
    scratch = [
        pltpu.VMEM((BAND, COLS), BF16),
        pltpu.VMEM((BAND, COLS), BF16),
        pltpu.VMEM((BAND, 131 * 128), BF16),
        pltpu.VMEM((BAND, 131 * 128), BF16),
        pltpu.VMEM((BAND * 32, 128), F32),
        pltpu.VMEM((IN_ROWS * 32, 128), F32),
        pltpu.VMEM((LON * IN_ROWS, 128), F32),
        pltpu.VMEM((LON * IN_ROWS, 128), F32),
        pltpu.VMEM((1, 128), F32),
        pltpu.VMEM((LON, 128), F32),
        pltpu.VMEM((OWN * 32, 1024), BF16),
        pltpu.VMEM((OWN * 32, 1024), BF16),
        pltpu.VMEM((OWN * 32, 1024), BF16),
        pltpu.VMEM((OWN * 32, 1024), BF16),
        pltpu.VMEM((LON * 48, 128), F32),
        pltpu.VMEM((256, 1024), BF16),
        pltpu.VMEM((OWN * 32, 128), F32),
        pltpu.VMEM((OUT_ROWS * 32, 128), F32),
        pltpu.VMEM((LON * SPACE, 128), F32),
        pltpu.VMEM((LON * SPACE, 128), F32),
        pltpu.VMEM(((OWN + 1) * 32, 128), BF16),
        pltpu.VMEM(((OWN + 1) * 32, 128), BF16),
        pltpu.VMEM((8, 32, WIDE), F32),
        pltpu.VMEM((8, 32, WIDE), F32),
        pltpu.VMEM((8, 32, WIDE), F32),
        pltpu.VMEM((2, 16, WIDE), F32),
        pltpu.VMEM((2, 16, WIDE), F32),
        pltpu.VMEM((2, 32, WIDE), F32),
        pltpu.VMEM((2, 32, WIDE), F32),
        pltpu.VMEM((2, 32, WIDE), F32),
        pltpu.VMEM((32, WIDE), F32),
        dma((2,)),
        dma((LON,)), dma((LON,)), dma((LON,)), dma((LON,)), dma((LON,)), dma((LON,)),
        dma((8,)), dma((8,)), dma((12,)), dma((12,)), dma((2,)), dma((2,)),
    ]
    return pl.pallas_call(
        kernel,
        out_shape=jax.ShapeDtypeStruct((LEV, SHARE), F32),
        in_specs=[vmem, vmem, vmem, smem, smem, hbm, hbm],
        out_specs=vmem,
        scratch_shapes=scratch,
        compiler_params=pltpu.CompilerParams(
            collective_id=0, has_side_effects=True, vmem_limit_bytes=60 * 1024 * 1024
        ),
    )(turned(wind_u), turned(wind_v), turned(vorticity), sample_level, slot_wavenumber,
      legendre_p, legendre_h)


def solution(mesh):
    placed = (
        P("lat", "lon", None),
        P("lat", "lon", None),
        P("lat", "lon", None),
        P(),
        P("lon"),
        P("lat", "lon"),
        P("lat", "lon"),
    )
    return jax.shard_map(
        body, mesh=mesh, in_specs=placed, out_specs=P(None, ("lon", "lat")), check_vma=False
    )
```

time: 73.7 us -> 62 us (0.84)
  the two profiles are of different devices: /device:TPU:72 before, /device:TPU:2 now
where the time goes in v2:
time: 62 us; the launch traced here: 61.8 us
  Pallas kernels  60.5 us (98%)
  local copies, waits for them, and re-layouts  1.3 us (2%)
    pallas_call x1, Pallas kernels, body(): pl.pallas_call(kernel, out_shape=jax.ShapeDtypeStruct((LEV, SHARE), F32),...  60.5 us
    unnamed x1, local copies, waits for them, and re-layouts  1.3 us

profile of v2, /device:TPU:2, one launch (start us, length us, event | category | flops | bytes accessed | tf_op | source)
XLA Modules:
  0.0 61.8 jit_solution(7984387669418678965)
XLA Ops:
  0.0 60.5 %shard_map.73 = f32[2,1035]{1,0:T(2,128)} custom-call(f32[45,16,45]{2,1,0:T(8,128)} %bitcast.3, f32[45,16,45]{2,1,0:T(8,128)} %bitcast.4, f32[45,16,45]{2,1,0:T(8,128)} %bitcast.5, s32[16]{0:T(128)} %level_ref.1, s32[23]{0:T(128)} %wave_ref.1, bf16[45,16560]{1,0:T(8,128)(2,1)} %p_hbm.1, bf16[45,16560]{1,0:T(8,128)(2,1)} %h_hbm.1), custom_call_target="tpu_custom_call" | custom-call | tf_op jit(solution)/shard_map/pallas_call | solution.py:526
  60.5 1.3 %copy.9 = f32[2,1035]{1,0:T(2,128)} copy(f32[2,1035]{1,0:T(2,128)} %shard_map.73) | data formatting | bytes 16560

commit v3 on v2

--- a/solution.py
+++ b/solution.py
@@ -24,7 +24,7 @@
 SPACE = 24
 COLS = OWN * MAXM
 SHARE = COLS // LAT
-WIDE = 1152
+TALL = 264
 STEP = 11
 
 F32 = jnp.float32
@@ -81,10 +81,10 @@
 
 
 def kernel(
-    u_ref, v_ref, z_ref, level_ref, wave_ref, p_hbm, h_hbm, out_ref,
-    p_ref, h_ref, wide_p, wide_h, flux, row1, send1, recv1, wsend, wrecv,
+    u_hbm, v_hbm, z_hbm, level_ref, wave_ref, p_hbm, h_hbm, out_ref,
+    u_ref, v_ref, z_ref, p_ref, h_ref, wide_p, wide_h, flux, row1, send1, recv1, wsend, wrecv,
     cos_hi, cos_lo, sin_hi, sin_lo, field, xs, coeff, row2, send2, recv2, left_p, left_h,
-    toward, held, got_core, got_a, got_b, plus, minus, final, got_z,
+    toward, held, got_core, got_far, plus, minus, final, got_z,
     load_sem, wsend_sem, wrecv_sem, send1_sem, recv1_sem, send2_sem, recv2_sem,
     core_send, core_recv, x_send, x_recv, z_send, z_recv,
 ):
@@ -105,10 +105,14 @@
     def other(k):
         return lax.rem(me + STEP * k, LON)
 
+    load_fields = [
+        pltpu.make_async_copy(src, dst, load_sem.at[2 + i])
+        for i, (src, dst) in enumerate(((z_hbm, z_ref), (u_hbm, u_ref), (v_hbm, v_ref)))
+    ]
+    for load in load_fields:
+        load.start()
     load_p = pltpu.make_async_copy(p_hbm, p_ref, load_sem.at[0])
     load_h = pltpu.make_async_copy(h_hbm, h_ref, load_sem.at[1])
-    load_p.start()
-    load_h.start()
     barrier = pltpu.get_barrier_semaphore()
 
     def greet(k, carry):
@@ -118,6 +122,9 @@
     lax.fori_loop(1, LON, greet, 0)
     for there in (partner, up, down, across):
         pl.semaphore_signal(barrier, inc=1, device_id=(me, there), device_id_type=MESH)
+
+    load_p.start()
+    load_h.start()
 
     rows16 = iota((S, 128), 0)
     upper = jnp.zeros((S, 128), F32)
@@ -125,7 +132,7 @@
         upper = jnp.where(rows16 == s, level_ref[s].astype(F32), upper)
     lower = 1.0 - upper
     upper45 = upper[None, :, :LOCAL]
-    lower45 = lower[None, :, :LOCAL]
+    is_upper = upper45 > 0.5
     STRIP = 9
 
     def eddies(strip, carry):
@@ -133,13 +140,13 @@
 
         def eddy(ref):
             value = ref[pl.ds(at, STRIP)]
-            one = jnp.sum(value * upper45, axis=1, keepdims=True)
-            zero = jnp.sum(value * lower45, axis=1, keepdims=True)
-            return value - (one * upper45 + zero * lower45) * (1.0 / DAYS)
+            high = value * upper45
+            one = jnp.sum(high, axis=1, keepdims=True) * (1.0 / DAYS)
+            zero = jnp.sum(value - high, axis=1, keepdims=True) * (1.0 / DAYS)
+            return value - jnp.where(is_upper, one, zero)
 
         row = lat * BAND + at + iota((STRIP, 1, LOCAL), 0)
-        theta = (row.astype(F32) + 0.5) * (math.pi / NLAT) - 0.5 * math.pi
-        ez = eddy(z_ref) * jnp.cos(theta)
+        ez = eddy(z_ref) * sincos(row.astype(F32) - (0.5 * NLAT - 0.5))[0]
         fu = eddy(u_ref) * ez
         fv = eddy(v_ref) * ez
         for j in range(STRIP):
@@ -148,6 +155,8 @@
             flux[pl.ds(base + S, S), 0:LOCAL] = fv[j]
         return carry
 
+    for load in load_fields:
+        load.wait()
     lax.fori_loop(0, BAND // STRIP, eddies, 0)
 
     for j in range(IN_ROWS):
@@ -274,7 +283,19 @@
 
     is_v = me >= S
     nt = (((1,), (1,)), ((), ()))
-    for first, count in ((0, 8), (8, 8), (16, 7)):
+    def out_block(c, first, count):
+        return pl.ds(pl.multiple_of(c * SPACE + first, 8), count)
+
+    def copy2(k, there, source, first, count, sem):
+        return pltpu.make_async_remote_copy(
+            src_ref=send2.at[out_block(k, first, count)],
+            dst_ref=recv2.at[out_block(source, first, count)],
+            send_sem=send2_sem.at[sem + k], recv_sem=recv2_sem.at[sem + source],
+            device_id=(there, lat), device_id_type=MESH,
+        )
+
+    parts = ((0, 12, 0, 8, 0), (12, 11, 8, OUT_ROWS - 8, LON))
+    for first, count, row, rows, sem in parts:
         size = count * 32
         at = slice(first * 32, first * 32 + size)
         low_part = iota((size, 128), 1) < 64
@@ -297,35 +318,27 @@
         far = jnp.where(low_part, roll64(s), c)
         coeff[at, :] = (near + sign * far) * jnp.where(low_part, sin_scale, cos_scale)
 
-    for j in range(OUT_ROWS):
-        row2[32 * j:32 * j + 32, :] = packed(
-            lambda t: (coeff[32 * (t // 2):32 * (t // 2) + 32, :], 64 * (t % 2)), 2 * OWN, j
-        )
-
-    def out_block(c):
-        return pl.ds(pl.multiple_of(c * SPACE, 8), OUT_ROWS)
-
-    def copy2(k, there, source):
-        return pltpu.make_async_remote_copy(
-            src_ref=send2.at[out_block(k)], dst_ref=recv2.at[out_block(source)],
-            send_sem=send2_sem.at[k], recv_sem=recv2_sem.at[source],
-            device_id=(there, lat), device_id_type=MESH,
-        )
-
-    def start2(k, carry):
-        o = other(k)
-        send2[out_block(k), :] = row2[pl.ds(o, OUT_ROWS, stride=32), :]
-        copy2(k, o, me).start()
-        return carry
-
-    lax.fori_loop(1, LON, start2, 0)
-    recv2[out_block(me), :] = row2[pl.ds(me, OUT_ROWS, stride=32), :]
-
-    def wait2(k, carry):
-        copy2(k, other(k), other(k)).wait()
-        return carry
-
-    lax.fori_loop(1, LON, wait2, 0)
+        for j in range(row, row + rows):
+            row2[32 * j:32 * j + 32, :] = packed(
+                lambda t: (coeff[32 * (t // 2):32 * (t // 2) + 32, :], 64 * (t % 2)), 2 * OWN, j
+            )
+
+        def start2(k, carry):
+            o = other(k)
+            send2[out_block(k, row, rows), :] = row2[pl.ds(32 * row + o, rows, stride=32), :]
+            copy2(k, o, me, row, rows, sem).start()
+            return carry
+
+        lax.fori_loop(1, LON, start2, 0)
+        recv2[out_block(me, row, rows), :] = row2[pl.ds(32 * row + me, rows, stride=32), :]
+
+    for first, count, row, rows, sem in parts:
+
+        def wait2(k, carry):
+            copy2(k, other(k), other(k), row, rows, sem).wait()
+            return carry
+
+        lax.fori_loop(1, LON, wait2, 0)
 
     out_tiles = {}
 
@@ -361,7 +374,17 @@
             turned += [pltpu.roll(r[:, :128], back, 1), pltpu.roll(r[:, 128:], back, 1)]
         return [jnp.where(inside, turned[i], turned[i + 1]) for i in range(9)]
 
-    order = [(1, 2), (1, 1), (1, 3), (0, 2), (1, 0), (0, 1), (0, 3), (0, 0)]
+    def put(ref, i, b):
+        pieces = chunk(b)
+        for n in range(8):
+            ref[i, 32 * n:32 * n + 32, :] = pieces[n]
+        last = pieces[8]
+        tail = last[0:8]
+        for g in range(1, 4):
+            tail = jnp.where(lane32[:8] < 32 * g, tail, pltpu.roll(last[8 * g:8 * g + 8], 32 * g, 1))
+        ref[i, 256:264, :] = tail
+
+    order = [(1, 2), (1, 1), (1, 3), (1, 0), (0, 2), (0, 1), (0, 3), (0, 0)]
     place = {pair: i for i, pair in enumerate(order)}
 
     def target(pair, cc):
@@ -377,106 +400,137 @@
     core_copies = {}
 
     def give(i):
-        pieces = chunk(target(order[i], 1 - core))
-        for n in range(9):
-            toward[i, :, 128 * n:128 * (n + 1)] = pieces[n]
+        put(toward, i, target(order[i], 1 - core))
         core_copies[i] = send(toward.at[i], got_core.at[i], core_send, core_recv, i, partner)
         core_copies[i].start()
 
     def keep_own(i):
-        pieces = chunk(target(order[i], core))
-        for n in range(9):
-            held[i, :, 128 * n:128 * (n + 1)] = pieces[n]
+        put(held, i, target(order[i], core))
 
     def merge(i):
         core_copies[i].wait()
         held[i] = held[i] + got_core[i]
 
-    A, B = slice(0, 16), slice(16, 32)
+    blocks = [
+        (1, slice(0, 64), slice(64, 128)),
+        (1, slice(128, 192), slice(192, TALL)),
+        (0, slice(0, 128), slice(128, TALL)),
+    ]
     x_copies = {}
 
     def x_start(i, src, dst, there):
         x_copies[i] = send(src, dst, x_send, x_recv, i, there)
         x_copies[i].start()
 
-    def far_start(dz):
+    def far_start(n):
+        dz, a, b = blocks[n]
         i = place[(dz, 2)]
-        x_start(6 * dz, held.at[i, A], got_a.at[dz], up)
-        x_start(6 * dz + 1, held.at[i, B], got_b.at[dz], down)
-
-    def near_start(dz):
-        x_start(6 * dz + 2, held.at[place[(dz, 1)], B], plus.at[dz, B], up)
-        x_start(6 * dz + 3, held.at[place[(dz, 3)], A], minus.at[dz, A], down)
-
-    def relay(dz):
+        x_start(6 * n, held.at[i, a], got_far.at[dz, a], up)
+        x_start(6 * n + 1, held.at[i, b], got_far.at[dz, b], down)
+
+    def near_start(n):
+        dz, a, b = blocks[n]
+        x_start(6 * n + 2, held.at[place[(dz, 1)], b], plus.at[dz, b], up)
+        x_start(6 * n + 3, held.at[place[(dz, 3)], a], minus.at[dz, a], down)
+
+    def relay(n):
+        dz, a, b = blocks[n]
         i, j = place[(dz, 1)], place[(dz, 3)]
-        x_copies[6 * dz].wait()
-        held[i, A] = held[i, A] + got_a[dz]
-        x_start(6 * dz + 4, held.at[i, A], plus.at[dz, A], up)
-        x_copies[6 * dz + 1].wait()
-        held[j, B] = held[j, B] + got_b[dz]
-        x_start(6 * dz + 5, held.at[j, B], minus.at[dz, B], down)
-
-    def finish(dz, part, one, two):
+        x_copies[6 * n].wait()
+        held[i, a] = held[i, a] + got_far[dz, a]
+        x_start(6 * n + 4, held.at[i, a], plus.at[dz, a], up)
+        x_copies[6 * n + 1].wait()
+        held[j, b] = held[j, b] + got_far[dz, b]
+        x_start(6 * n + 5, held.at[j, b], minus.at[dz, b], down)
+
+    def finish(n):
+        dz, a, b = blocks[n]
         own = place[(dz, 0)]
-        x_copies[6 * dz + one].wait()
-        x_copies[6 * dz + two].wait()
-        final[dz, part] = held[own, part] + plus[dz, part] + minus[dz, part]
-
-    for i in range(4):
-        give(i)
+        for part, one, two in ((a, 3, 4), (b, 2, 5)):
+            x_copies[6 * n + one].wait()
+            x_copies[6 * n + two].wait()
+            final[dz, part] = held[own, part] + plus[dz, part] + minus[dz, part]
+
+    z_copies = []
+
+    def z_start(n):
+        part = slice(blocks[n][1].start, blocks[n][2].stop)
+        copy = send(final.at[1, part], got_z.at[part], z_send, z_recv, n, across)
+        copy.start()
+        z_copies.append(copy)
+
+    give(0)
+    give(1)
+    give(2)
     keep_own(0)
     merge(0)
-    far_start(1)
+    far_start(0)
     keep_own(1)
     merge(1)
     keep_own(2)
     merge(2)
+    near_start(0)
+    far_start(1)
+    give(3)
+    give(4)
+    keep_own(3)
+    relay(0)
     near_start(1)
-    for i in range(4, 8):
-        give(i)
-    keep_own(3)
+    give(5)
+    give(6)
     keep_own(4)
+    merge(4)
     relay(1)
+    far_start(2)
+    give(7)
     merge(3)
-    far_start(0)
-    merge(4)
     keep_own(5)
+    keep_own(6)
     merge(5)
-    keep_own(6)
     merge(6)
-    near_start(0)
+    finish(0)
+    z_start(0)
+    near_start(2)
+    finish(1)
+    z_start(1)
     keep_own(7)
     merge(7)
-    finish(1, A, 3, 4)
-    z_a = send(final.at[1, A], got_z.at[A], z_send, z_recv, 0, across)
-    z_a.start()
-    finish(1, B, 2, 5)
-    z_b = send(final.at[1, B], got_z.at[B], z_send, z_recv, 1, across)
-    z_b.start()
-    relay(0)
-    finish(0, A, 3, 4)
-    finish(0, B, 2, 5)
-
-    first = lat * SHARE
-    slot = first // MAXM
-    lane = first + iota((1, WIDE), 1)
-    keep = jnp.zeros((1, WIDE), F32)
-    for d in range(3):
-        q = jnp.minimum(slot + d, OWN - 1)
-        wave = wave_ref[q]
-        n = lane - (slot + d) * MAXM
-        good = (n >= 0) & (n < MAXM) & (n >= wave) & (wave >= 0)
-        keep = jnp.where(good, 1.0 / DAYS, keep)
-    z_a.wait()
-    re = final[0, A] + got_z[A]
-    z_b.wait()
-    im = final[0, B] + got_z[B]
-    power = re * re + im * im
-    one = jnp.sum(power * upper[:, :1], axis=0, keepdims=True)
-    zero = jnp.sum(power * lower[:, :1], axis=0, keepdims=True)
-    out_ref[0:1, :] = (zero * keep)[:, :SHARE]
-    out_ref[1:2, :] = (one * keep)[:, :SHARE]
+    relay(2)
+    finish(2)
+
+    column = lat * SHARE
+    slot = column // MAXM
+
+    def power(n):
+        count = SHARE - 1024 if n == 8 else 128
+        if n < 8:
+            value = final[0, 32 * n:32 * n + 32] + got_z[32 * n:32 * n + 32]
+        else:
+            tail = final[0, 256:TALL] + got_z[256:TALL]
+            value = jnp.concatenate(
+                [tail] + [pltpu.roll(tail, 128 - 32 * g, 1) for g in range(1, 4)], axis=0
+            )
+        lane = column + 128 * n + iota((1, 128), 1)
+        keep = jnp.zeros((1, 128), F32)
+        for d in range(3):
+            q = jnp.minimum(slot + d, OWN - 1)
+            wave = wave_ref[q]
+            degree = lane - (slot + d) * MAXM
+            good = (degree >= 0) & (degree < MAXM) & (degree >= wave) & (wave >= 0)
+            keep = jnp.where(good, 1.0 / DAYS, keep)
+        square = value[:S] * value[:S] + value[S:] * value[S:]
+        one = jnp.sum(square * upper, axis=0, keepdims=True) * keep
+        zero = jnp.sum(square * lower, axis=0, keepdims=True) * keep
+        lanes = slice(128 * n, 128 * n + count)
+        out_ref[0:1, lanes] = zero[:, :count]
+        out_ref[1:2, lanes] = one[:, :count]
+
+    z_copies[0].wait()
+    for n in range(4):
+        power(n)
+    z_copies[1].wait()
+    for n in range(4, 9):
+        power(n)
 
 
 def body(wind_u, wind_v, vorticity, sample_level, slot_wavenumber, legendre_p, legendre_h):
@@ -487,7 +541,9 @@
     smem = pl.BlockSpec(memory_space=pltpu.SMEM)
     hbm = pl.BlockSpec(memory_space=pl.ANY)
     dma = pltpu.SemaphoreType.DMA
+    block = pltpu.VMEM((BAND, S, LOCAL), F32)
     scratch = [
+        block, block, block,
         pltpu.VMEM((BAND, COLS), BF16),
         pltpu.VMEM((BAND, COLS), BF16),
         pltpu.VMEM((BAND, 131 * 128), BF16),
@@ -510,23 +566,22 @@
         pltpu.VMEM((LON * SPACE, 128), F32),
         pltpu.VMEM(((OWN + 1) * 32, 128), BF16),
         pltpu.VMEM(((OWN + 1) * 32, 128), BF16),
-        pltpu.VMEM((8, 32, WIDE), F32),
-        pltpu.VMEM((8, 32, WIDE), F32),
-        pltpu.VMEM((8, 32, WIDE), F32),
-        pltpu.VMEM((2, 16, WIDE), F32),
-        pltpu.VMEM((2, 16, WIDE), F32),
-        pltpu.VMEM((2, 32, WIDE), F32),
-        pltpu.VMEM((2, 32, WIDE), F32),
-        pltpu.VMEM((2, 32, WIDE), F32),
-        pltpu.VMEM((32, WIDE), F32),
-        dma((2,)),
-        dma((LON,)), dma((LON,)), dma((LON,)), dma((LON,)), dma((LON,)), dma((LON,)),
-        dma((8,)), dma((8,)), dma((12,)), dma((12,)), dma((2,)), dma((2,)),
+        pltpu.VMEM((8, TALL, 128), F32),
+        pltpu.VMEM((8, TALL, 128), F32),
+        pltpu.VMEM((8, TALL, 128), F32),
+        pltpu.VMEM((2, TALL, 128), F32),
+        pltpu.VMEM((2, TALL, 128), F32),
+        pltpu.VMEM((2, TALL, 128), F32),
+        pltpu.VMEM((2, TALL, 128), F32),
+        pltpu.VMEM((TALL, 128), F32),
+        dma((5,)),
+        dma((LON,)), dma((LON,)), dma((LON,)), dma((LON,)), dma((2 * LON,)), dma((2 * LON,)),
+        dma((8,)), dma((8,)), dma((18,)), dma((18,)), dma((2,)), dma((2,)),
     ]
     return pl.pallas_call(
         kernel,
         out_shape=jax.ShapeDtypeStruct((LEV, SHARE), F32),
-        in_specs=[vmem, vmem, vmem, smem, smem, hbm, hbm],
+        in_specs=[hbm, hbm, hbm, smem, smem, hbm, hbm],
         out_specs=vmem,
         scratch_shapes=scratch,
         compiler_params=pltpu.CompilerParams(

time: 62 us -> 62.2 us (level)
  the two profiles are of different devices: /device:TPU:2 before, /device:TPU:1 now
where the time goes in v3:
time: 62.2 us; the launch traced here: 62.1 us
  Pallas kernels  60.8 us (98%)
  local copies, waits for them, and re-layouts  1.3 us (2%)
    pallas_call x1, Pallas kernels, body(): pl.pallas_call(kernel, out_shape=jax.ShapeDtypeStruct((LEV, SHARE), F32),...  60.8 us
    unnamed x1, local copies, waits for them, and re-layouts  1.3 us

profile of v3, /device:TPU:1, one launch (start us, length us, event | category | flops | bytes accessed | tf_op | source)
XLA Modules:
  0.0 62.1 jit_solution(7429767722648225497)
XLA Ops:
  0.0 60.8 %shard_map.73 = f32[2,1035]{1,0:T(2,128)} custom-call(f32[45,16,45]{2,1,0:T(8,128)} %bitcast.3, f32[45,16,45]{2,1,0:T(8,128)} %bitcast.4, f32[45,16,45]{2,1,0:T(8,128)} %bitcast.5, s32[16]{0:T(128)} %level_ref.1, s32[23]{0:T(128)} %wave_ref.1, bf16[45,16560]{1,0:T(8,128)(2,1)} %p_hbm.1, bf16[45,16560]{1,0:T(8,128)(2,1)} %h_hbm.1), custom_call_target="tpu_custom_call" | custom-call | tf_op jit(solution)/shard_map/pallas_call | solution.py:581
  60.8 1.3 %copy.9 = f32[2,1035]{1,0:T(2,128)} copy(f32[2,1035]{1,0:T(2,128)} %shard_map.73) | data formatting | bytes 16560

commit v4 on v3

--- a/solution.py
+++ b/solution.py
@@ -25,6 +25,7 @@
 COLS = OWN * MAXM
 SHARE = COLS // LAT
 TALL = 264
+UNROLL = 31
 STEP = 11
 
 F32 = jnp.float32
@@ -119,7 +120,7 @@
         pl.semaphore_signal(barrier, inc=1, device_id=(other(k), lat), device_id_type=MESH)
         return carry
 
-    lax.fori_loop(1, LON, greet, 0)
+    lax.fori_loop(1, LON, greet, 0, unroll=UNROLL)
     for there in (partner, up, down, across):
         pl.semaphore_signal(barrier, inc=1, device_id=(me, there), device_id_type=MESH)
 
@@ -182,7 +183,7 @@
         wave_copy(k, other(k), me).start()
         return carry
 
-    lax.fori_loop(1, LON, wave_start, 0)
+    lax.fori_loop(1, LON, wave_start, 0, unroll=UNROLL)
 
     def in_block(c):
         return pl.ds(pl.multiple_of(c * IN_ROWS, 8), IN_ROWS)
@@ -200,7 +201,7 @@
         copy1(k, c, me).start()
         return carry
 
-    lax.fori_loop(1, LON, start1, 0)
+    lax.fori_loop(1, LON, start1, 0, unroll=UNROLL)
     recv1[in_block(me), :] = row1[pl.ds(me, IN_ROWS, stride=32), :]
 
     load_p.wait()
@@ -222,7 +223,7 @@
         wave_copy(k, other(k), other(k)).wait()
         return carry
 
-    lax.fori_loop(1, LON, wave_wait, 0)
+    lax.fori_loop(1, LON, wave_wait, 0, unroll=UNROLL)
     lane32 = iota((32, 128), 1)
 
     def wave_column(q):
@@ -256,7 +257,7 @@
         copy1(k, other(k), other(k)).wait()
         return carry
 
-    lax.fori_loop(1, LON, wait1, 0)
+    lax.fori_loop(1, LON, wait1, 0, unroll=UNROLL)
 
     row_tile = {}
 
@@ -329,7 +330,7 @@
             copy2(k, o, me, row, rows, sem).start()
             return carry
 
-        lax.fori_loop(1, LON, start2, 0)
+        lax.fori_loop(1, LON, start2, 0, unroll=UNROLL)
         recv2[out_block(me, row, rows), :] = row2[pl.ds(32 * row + me, rows, stride=32), :]
 
     for first, count, row, rows, sem in parts:
@@ -338,7 +339,7 @@
             copy2(k, other(k), other(k), row, rows, sem).wait()
             return carry
 
-        lax.fori_loop(1, LON, wait2, 0)
+        lax.fori_loop(1, LON, wait2, 0, unroll=UNROLL)
 
     out_tiles = {}
 
@@ -459,42 +460,40 @@
         copy.start()
         z_copies.append(copy)
 
-    give(0)
-    give(1)
-    give(2)
+    for i in range(4):
+        give(i)
     keep_own(0)
+    give(4)
+    keep_own(1)
+    give(5)
+    keep_own(2)
+    give(6)
+    give(7)
     merge(0)
     far_start(0)
-    keep_own(1)
     merge(1)
-    keep_own(2)
     merge(2)
     near_start(0)
     far_start(1)
-    give(3)
-    give(4)
     keep_own(3)
+    merge(3)
+    keep_own(4)
+    merge(4)
+    keep_own(5)
+    merge(5)
+    keep_own(6)
+    merge(6)
     relay(0)
     near_start(1)
-    give(5)
-    give(6)
-    keep_own(4)
-    merge(4)
     relay(1)
     far_start(2)
-    give(7)
-    merge(3)
-    keep_own(5)
-    keep_own(6)
-    merge(5)
-    merge(6)
+    near_start(2)
+    keep_own(7)
+    merge(7)
     finish(0)
     z_start(0)
-    near_start(2)
     finish(1)
     z_start(1)
-    keep_own(7)
-    merge(7)
     relay(2)
     finish(2)
 

time: 62.2 us -> 60.3 us (0.969)
  Pallas kernels: 60.8 us -> 58.8 us
    pallas_call x1, Pallas kernels: 60.8 us -> 58.8 us  [body(): pl.pallas_call(kernel, out_shape=jax.ShapeDtypeStruct((LEV, SHARE), F32),...]
where the time goes in v4:
time: 60.3 us; the launch traced here: 60.1 us
  Pallas kernels  58.8 us (98%)
  local copies, waits for them, and re-layouts  1.3 us (2%)
    pallas_call x1, Pallas kernels, body(): pl.pallas_call(kernel, out_shape=jax.ShapeDtypeStruct((LEV, SHARE), F32),...  58.8 us
    unnamed x1, local copies, waits for them, and re-layouts  1.3 us

profile of v4, /device:TPU:1, one launch (start us, length us, event | category | flops | bytes accessed | tf_op | source)
XLA Modules:
  0.0 60.1 jit_solution(5369078961207483985)
XLA Ops:
  0.0 58.8 %shard_map.73 = f32[2,1035]{1,0:T(2,128)} custom-call(f32[45,16,45]{2,1,0:T(8,128)} %bitcast.3, f32[45,16,45]{2,1,0:T(8,128)} %bitcast.4, f32[45,16,45]{2,1,0:T(8,128)} %bitcast.5, s32[16]{0:T(128)} %level_ref.1, s32[23]{0:T(128)} %wave_ref.1, bf16[45,16560]{1,0:T(8,128)(2,1)} %p_hbm.1, bf16[45,16560]{1,0:T(8,128)(2,1)} %h_hbm.1), custom_call_target="tpu_custom_call" | custom-call | tf_op jit(solution)/shard_map/pallas_call | solution.py:580
  58.8 1.3 %copy.9 = f32[2,1035]{1,0:T(2,128)} copy(f32[2,1035]{1,0:T(2,128)} %shard_map.73) | data formatting | bytes 16560

commit v5 on v4

--- a/solution.py
+++ b/solution.py
@@ -462,29 +462,26 @@
 
     for i in range(4):
         give(i)
-    keep_own(0)
-    give(4)
-    keep_own(1)
-    give(5)
-    keep_own(2)
-    give(6)
-    give(7)
+    for i in range(3):
+        keep_own(i)
     merge(0)
     far_start(0)
     merge(1)
     merge(2)
     near_start(0)
     far_start(1)
+    for i in range(4, 8):
+        give(i)
     keep_own(3)
     merge(3)
     keep_own(4)
+    relay(0)
+    near_start(1)
     merge(4)
     keep_own(5)
     merge(5)
     keep_own(6)
     merge(6)
-    relay(0)
-    near_start(1)
     relay(1)
     far_start(2)
     near_start(2)

time: 60.3 us -> 60 us (level)
  no operation moved by 1% of the time
where the time goes in v5:
time: 60 us; the launch traced here: 59.8 us
  Pallas kernels  58.5 us (98%)
  local copies, waits for them, and re-layouts  1.3 us (2%)
    pallas_call x1, Pallas kernels, body(): pl.pallas_call(kernel, out_shape=jax.ShapeDtypeStruct((LEV, SHARE), F32),...  58.5 us
    unnamed x1, local copies, waits for them, and re-layouts  1.3 us

profile of v5, /device:TPU:1, one launch (start us, length us, event | category | flops | bytes accessed | tf_op | source)
XLA Modules:
  0.0 59.8 jit_solution(13680060438546458612)
XLA Ops:
  0.0 58.5 %shard_map.73 = f32[2,1035]{1,0:T(2,128)} custom-call(f32[45,16,45]{2,1,0:T(8,128)} %bitcast.3, f32[45,16,45]{2,1,0:T(8,128)} %bitcast.4, f32[45,16,45]{2,1,0:T(8,128)} %bitcast.5, s32[16]{0:T(128)} %level_ref.1, s32[23]{0:T(128)} %wave_ref.1, bf16[45,16560]{1,0:T(8,128)(2,1)} %p_hbm.1, bf16[45,16560]{1,0:T(8,128)(2,1)} %h_hbm.1), custom_call_target="tpu_custom_call" | custom-call | tf_op jit(solution)/shard_map/pallas_call | solution.py:577
  58.5 1.3 %copy.9 = f32[2,1035]{1,0:T(2,128)} copy(f32[2,1035]{1,0:T(2,128)} %shard_map.73) | data formatting | bytes 16560
